TPU v7x, 256 devices: a whole 4x4x8 slice. The times are simulated.
256 devices in a mesh: dp: 64 (over z, y, core), tensor: 4 (over x).
Axes of the slice: x: 4, y: 4, z: 8, core: 2. Of those that a mesh axis runs over, the one named last changes fastest.
Arguments:
- tokens: bfloat16 [32768, 8192], P('dp', 'tensor'), may hold values from -6 to 6
- token_adapter_index: int32 [32768, 1], P('dp'), may hold values from 0 to 63; in each aligned block of 512 rows (0 to 511, 512 to 1023, ...) at most 16 rows name the same one
- frozen_key_value_weight: bfloat16 [8192, 2048], P('tensor'), may hold values from -0.0625 to 0.0625
- adapter_down_weight: bfloat16 [64, 64, 8192], P('dp', None, 'tensor'), may hold values from -0.0625 to 0.0625
- adapter_up_weight: bfloat16 [64, 64, 2048], P('dp', None, 'tensor'), may hold values from -0.75 to 0.75
Outputs:
- projected: bfloat16 [32768, 2048], P('dp', 'tensor')
Inputs may be any that keep to these rules, and one draw needn't show every extreme that they name: `token_adapter_index`: among the tokens of one index of dp, no adapter is named by more than 16 tokens, a bound that some block reaches.
All inputs are finite; a program needn't handle non-finite values.
Results may differ from a plain program's by a relative error of at most 0.0048.
Values may be sent and summed in bfloat16 or wider, within the bound.
No kernel may reach another device: no remote copies, remote signals or barrier semaphores. Data moves between devices by JAX's collectives and lax.ppermute only.
A program may use at most 128 MiB of HBM per device.

v0:
```python
import jax
import jax.numpy as jnp
from jax import lax
from jax.sharding import PartitionSpec as P


def on_device(
    tokens, token_adapter_index, frozen_key_value_weight, adapter_down_weight, adapter_up_weight
):
    holder_count = lax.axis_size("dp")
    token_count = tokens.shape[0]
    feature_count = tokens.shape[1]
    row_capacity = 2 * token_count // holder_count
    adapter_rank_width = adapter_down_weight.shape[1]
    adapter_of = token_adapter_index[:, 0]
    membership = (adapter_of[:, None] == jnp.arange(holder_count, dtype=jnp.int32)[None, :]).astype(
        jnp.int32
    )
    earlier = jnp.cumsum(membership, axis=0) - membership
    position = jnp.sum(earlier * membership, axis=1)
    adapter_slot_index = adapter_of * row_capacity + position
    send_buffer = (
        jnp.zeros((holder_count * row_capacity, feature_count), tokens.dtype)
        .at[adapter_slot_index]
        .set(tokens)
    )
    send_buffer = send_buffer.reshape(holder_count, row_capacity, feature_count)
    partial_value = jnp.dot(tokens, frozen_key_value_weight, preferred_element_type=jnp.float32)
    base_out = lax.psum_scatter(partial_value, "tensor", scatter_dimension=1, tiled=True)
    product = jnp.einsum(
        "acd,ard->acr",
        send_buffer,
        lax.all_gather(adapter_down_weight, "dp", axis=0, tiled=True),
        preferred_element_type=jnp.float32,
    )
    summed = lax.psum(product.reshape(holder_count, row_capacity * adapter_rank_width), "tensor")
    reduced_activations = summed.reshape(holder_count, row_capacity, adapter_rank_width).astype(
        jnp.bfloat16
    )
    adapter_delta = jnp.einsum(
        "flz,fzq->flq",
        reduced_activations,
        lax.all_gather(adapter_up_weight, "dp", axis=0, tiled=True),
        preferred_element_type=jnp.float32,
    ).astype(jnp.bfloat16)
    flattened_delta = adapter_delta.reshape(holder_count * row_capacity, adapter_delta.shape[2])[
        adapter_slot_index
    ]
    return (base_out + flattened_delta.astype(jnp.float32)).astype(jnp.bfloat16)


def solution(mesh):
    placed = (
        P("dp", "tensor"),
        P("dp", None),
        P("tensor", None),
        P("dp", None, "tensor"),
        P("dp", None, "tensor"),
    )
    return jax.shard_map(
        on_device, mesh=mesh, in_specs=placed, out_specs=P("dp", "tensor"), check_vma=False
    )
```

profile of v0, /device:TPU:1, one launch (start us, length us, event | category | flops | bytes accessed | tf_op | source)
XLA Modules:
  0.0 209.0 jit_solution(12527318570697684783)
XLA Ops:
  7.4 0.0 all-gather.3.cloned.1.call-start
  7.4 0.7 all-gather.3.cloned.1.call-update
  8.1 0.0 all-gather.5.cloned.1.call-start
  8.1 0.7 all-gather.5.cloned.1.call-update
  8.8 0.0 reduce-scatter.2.cloned.1.call-start
  8.9 10.5 %fusion.6 = f32[512,2048]{1,0:T(8,128)} fusion(bf16[512,2048]{1,0:T(8,128)(2,1)} %param.5, bf16[2048,2048]{1,0:T(8,128)(2,1)} %param.7), kind=kOutput, calls=%fused_computation.17 | convolution fusion | flops 4294967296 | bytes 14680064 | tf_op jit(solution)/shard_map/dot_general | solution.py:28
  19.4 0.0 copy-start
  19.4 0.0 reduce-scatter.2.cloned.1.call-update
  19.4 0.7 copy-done
  20.1 1.2 reduce-window.6
  21.3 0.2 slice_reduce_fusion
  21.5 0.1 fusion.4
  21.7 7.3 %scatter_custom_fusion = bf16[1024,2048]{1,0:T(8,128)(2,1)} fusion(s32[512]{0:T(512)S(1)} %bitcast.36, bf16[512,2048]{1,0:T(8,128)(2,1)} %param.5, bf16[]{:T(256)} %constant.4.clone.1), kind=kCustom, calls=%fused_computation.2 | custom fusion | bytes 4194816 | tf_op jit(solution)/shard_map/scatter | solution.py:25
  29.0 86.4 %all-gather.3.cloned.1.call-done = bf16[64,64,2048]{2,1,0:T(8,128)(2,1)} async-done(((bf16[1,64,2048]{2,1,0:T(8,128)(2,1)}), bf16[64,64,2048]{2,1,0:T(8,128)(2,1)}) %all-gather.3.cloned.1.call-update) | async-done | bytes 16777232 | tf_op jit(solution)/shard_map/all_gather | solution.py:33
  115.4 11.5 %fusion.7 = f32[64,16,64]{2,1,0:T(8,128)S(1)} fusion(bf16[64,16,2048]{2,1,0:T(8,128)(2,1)} %bitcast.32, bf16[64,64,2048]{2,1,0:T(8,128)(2,1)} %all-gather.3.cloned.1.call-done), kind=kOutput, calls=%fused_computation.18 | convolution fusion | flops 268435456 | bytes 21233664 | tf_op jit(solution)/shard_map/acd,ard->acr/dot_general | solution.py:30
  126.9 0.2 reshape.30
  127.0 16.6 %all-reduce.1 = bf16[64,1024]{1,0:T(8,128)(2,1)S(1)} all-reduce(f32[64,1024]{1,0:T(8,128)S(1)} %reshape.30), channel_id=1, replica_groups=mesh['dp'=64,'tensor'=4] {'tensor'}, use_global_device_ids=true, to_apply=%region_5.6 | all-reduce | flops 65536 | bytes 393216 | tf_op jit(solution)/shard_map/psum | solution.py:36
  143.7 0.2 convert_element_type.25
  143.9 50.7 %all-gather.5.cloned.1.call-done = bf16[64,64,512]{2,1,0:T(8,128)(2,1)} async-done(((bf16[1,64,512]{2,1,0:T(8,128)(2,1)}), bf16[64,64,512]{2,1,0:T(8,128)(2,1)}) %all-gather.5.cloned.1.call-update) | async-done | bytes 4194320 | tf_op jit(solution)/shard_map/all_gather | solution.py:43
  194.6 2.8 %convolution_convert_fusion = bf16[64,16,512]{2,1,0:T(8,128)(2,1)S(1)} fusion(bf16[64,16,64]{2,1,0:T(8,128)(2,1)S(1)} %convert_element_type.25, bf16[64,64,512]{2,1,0:T(8,128)(2,1)} %all-gather.5.cloned.1.call-done), kind=kOutput, calls=%fused_computation.4 | convolution fusion | flops 67633152 | bytes 5373952 | tf_op jit(solution)/shard_map/flz,fzq->flq/dot_general | solution.py:40
  197.4 2.0 gather_fusion
  199.4 0.0 reduce-scatter.2.cloned.1.call-done
  199.4 2.2 %add_convert_fusion = bf16[512,512]{1,0:T(8,128)(2,1)} fusion(f32[512,512]{1,0:T(8,128)} %reduce-scatter.2.cloned.1.call-done, bf16[512,512]{1,0:T(8,128)(2,1)S(1)} %gather_fusion), kind=kLoop, calls=%fused_computation.5 | loop fusion | flops 786432 | bytes 2097152 | tf_op jit(solution)/shard_map/convert_element_type | solution.py:49
  (5 shorter events, 0.1 us)
Async XLA Ops:
  7.4 108.0 %all-gather.3.cloned.1.call-start = ((), (), s32[]{:S(2)}) async-start(), calls=%async_computation.2 | async-start | bytes 17039360 | tf_op jit(solution)/shard_map/all_gather | solution.py:33
  8.1 186.5 %all-gather.5.cloned.1.call-start = ((), (), s32[]{:S(2)}) async-start(), calls=%async_computation.3 | async-start | bytes 4259840 | tf_op jit(solution)/shard_map/all_gather | solution.py:43
  8.8 190.6 %reduce-scatter.2.cloned.1.call-start = ((), (), s32[]{:S(2)}) async-start(), calls=%async_computation.1 | async-start | bytes 5242880 | tf_op jit(solution)/shard_map/reduce_scatter | solution.py:29
  19.4 0.7 copy-start
Sparse Core Ops, SparseCore 0:
  11.3 103.9 all-gather.2
  118.5 76.0 all-gather.4
Sparse Core Ops, SparseCore 1:
  19.5 53.0 reduce-scatter.1
where the time goes:
time: 209 us
  waiting for transfers between devices  139 us (67%)
  matrix products  24.8 us (12%)
  blocking collectives  16.6 us (8%)
  between operations  14.9 us (7%)
  local copies, waits for them, and re-layouts  10.5 us (5%)
  other arithmetic  3.57 us (2%)
    all_gather x1, waiting for transfers between devices, on_device(): lax.all_gather(adapter_down_weight, 'dp', axis=0, tiled=True)  86.4 us
    all_gather x1, waiting for transfers between devices, on_device(): lax.all_gather(adapter_up_weight, 'dp', axis=0, tiled=True)  50.7 us
    psum x1, blocking collectives, on_device(): lax.psum(product.reshape(holder_count, row_capacity * adapter_rank_width)...  16.6 us
    dot_general x1, matrix products, on_device(): jnp.einsum('acd,ard->acr', send_buffer, lax.all_gather(adapter_down_weigh...  11.5 us
    dot_general x1, matrix products, on_device(): jnp.dot(tokens, frozen_key_value_weight, preferred_element_type=jnp.float32)  10.5 us
    scatter x1, local copies, waits for them, and re-layouts, on_device(): send_buffer = jnp.zeros((holder_count * row_capacity, feature_count), tok...  7.26 us
  transfers between devices with their start and end apart: 3, of which 2 were waited for; matrix products, arithmetic and copies ran while one was open for 17% of the time, Pallas kernels for 0%

commit v1 on v0

--- a/solution.py
+++ b/solution.py
@@ -33,7 +33,10 @@
         lax.all_gather(adapter_down_weight, "dp", axis=0, tiled=True),
         preferred_element_type=jnp.float32,
     )
-    summed = lax.psum(product.reshape(holder_count, row_capacity * adapter_rank_width), "tensor")
+    summed = jnp.sum(
+        lax.all_gather(product.reshape(holder_count, row_capacity * adapter_rank_width), "tensor"),
+        axis=0,
+    )
     reduced_activations = summed.reshape(holder_count, row_capacity, adapter_rank_width).astype(
         jnp.bfloat16
     )

time: 209 us -> 290 us (1.39)
  waiting for transfers between devices: 139 us -> 235 us
  blocking collectives: 16.6 us -> 0 us
  other arithmetic: 3.57 us -> 6.92 us
    reduce_scatter x1, waiting for transfers between devices: 0.03 us -> 43.8 us  [on_device(): lax.psum_scatter(partial_value, 'tensor', scatter_dimension=1, tiled=True)]
    all_gather x1, waiting for transfers between devices: 50.7 us -> 82 us  [on_device(): lax.all_gather(adapter_up_weight, 'dp', axis=0, tiled=True)]
    psum x1 -> x0, blocking collectives: 16.6 us -> none  [on_device(): lax.psum(product.reshape(holder_count, row_capacity * adapter_rank_width)...]
    all_gather x0 -> x1, waiting for transfers between devices: none -> 11.8 us  [on_device(): lax.all_gather(product.reshape(holder_count, row_capacity * adapter_rank_...]
    all_gather x1, waiting for transfers between devices: 86.4 us -> 96.1 us  [on_device(): lax.all_gather(adapter_down_weight, 'dp', axis=0, tiled=True)]
  transfers between devices with their start and end apart: 3 -> 4, of which waited for: 2 -> 4; matrix products, arithmetic and copies ran while one was open for 17% -> 9% of each run, Pallas kernels for 0% -> 0%
where the time goes in v1:
time: 290 us
  waiting for transfers between devices  235 us (81%)
  matrix products  24 us (8%)
  between operations  13.2 us (5%)
  local copies, waits for them, and re-layouts  10.5 us (4%)
  other arithmetic  6.92 us (2%)
    all_gather x1, waiting for transfers between devices, on_device(): lax.all_gather(adapter_down_weight, 'dp', axis=0, tiled=True)  96.1 us
    all_gather x1, waiting for transfers between devices, on_device(): lax.all_gather(adapter_up_weight, 'dp', axis=0, tiled=True)  82 us
    reduce_scatter x1, waiting for transfers between devices, on_device(): lax.psum_scatter(partial_value, 'tensor', scatter_dimension=1, tiled=True)  43.8 us
    all_gather x1, waiting for transfers between devices, on_device(): lax.all_gather(product.reshape(holder_count, row_capacity * adapter_rank_...  11.8 us
    dot_general x1, matrix products, on_device(): jnp.einsum('acd,ard->acr', send_buffer, lax.all_gather(adapter_down_weigh...  11.6 us
    dot_general x1, matrix products, on_device(): jnp.dot(tokens, frozen_key_value_weight, preferred_element_type=jnp.float32)  9.48 us
    scatter x1, local copies, waits for them, and re-layouts, on_device(): send_buffer = jnp.zeros((holder_count * row_capacity, feature_count), tok...  7.2 us
  transfers between devices with their start and end apart: 4, of which 4 were waited for; matrix products, arithmetic and copies ran while one was open for 9% of the time, Pallas kernels for 0%

profile of v1, /device:TPU:1, one launch (start us, length us, event | category | flops | bytes accessed | tf_op | source)
XLA Modules:
  0.0 290.1 jit_solution(17994868904363144154)
XLA Ops:
  6.5 0.7 all-gather.4.cloned.1.call-update
  7.3 0.0 all-gather.6.cloned.1.call-start
  7.3 0.7 fusion.5
  8.0 1.2 reduce-window.6
  9.2 0.2 slice_reduce_fusion
  9.5 0.8 fusion.4
  10.3 0.7 compare_select_fusion
  11.0 7.2 %scatter_custom_fusion = bf16[1024,2048]{1,0:T(8,128)(2,1)} fusion(s32[512]{0:T(512)S(1)} %bitcast.36, bf16[512,2048]{1,0:T(8,128)(2,1)} %param.5, bf16[]{:T(256)} %constant.5.clone.1), kind=kCustom, calls=%fused_computation.2 | custom fusion | bytes 4194816 | tf_op jit(solution)/shard_map/scatter | solution.py:25
  18.2 96.1 %all-gather.4.cloned.1.call-done = bf16[64,64,2048]{2,1,0:T(8,128)(2,1)} async-done(((bf16[1,64,2048]{2,1,0:T(8,128)(2,1)}), bf16[64,64,2048]{2,1,0:T(8,128)(2,1)}) %all-gather.4.cloned.1.call-update) | async-done | bytes 16777232 | tf_op jit(solution)/shard_map/all_gather | solution.py:33
  114.3 11.6 %fusion.7 = f32[64,16,64]{2,1,0:T(8,128)S(1)} fusion(bf16[64,16,2048]{2,1,0:T(8,128)(2,1)} %bitcast.32, bf16[64,64,2048]{2,1,0:T(8,128)(2,1)} %all-gather.4.cloned.1.call-done), kind=kOutput, calls=%fused_computation.18 | convolution fusion | flops 268435456 | bytes 21233664 | tf_op jit(solution)/shard_map/acd,ard->acr/dot_general | solution.py:30
  126.0 0.9 all_gather_reshape.3
  126.8 0.0 all-gather.6.cloned.1.call-update
  126.9 0.0 all-gather.8.cloned.1.call-start
  126.9 0.7 all-gather.8.cloned.1.call-update
  127.6 0.2 reduce-scatter.2.cloned.1.call-start
  127.8 9.5 %fusion.6 = f32[512,2048]{1,0:T(8,128)} fusion(bf16[512,2048]{1,0:T(8,128)(2,1)S(1)} %copy-done, bf16[2048,2048]{1,0:T(8,128)(2,1)} %param.7), kind=kOutput, calls=%fused_computation.17 | convolution fusion | flops 4294967296 | bytes 14680064 | tf_op jit(solution)/shard_map/dot_general | solution.py:28
  137.4 11.8 %all-gather.6.cloned.1.call-done = f32[4,64,1024]{2,1,0:T(8,128)} async-done(((f32[1,64,1024]{2,1,0:T(8,128)}), f32[4,64,1024]{2,1,0:T(8,128)}) %all-gather.6.cloned.1.call-update) | async-done | bytes 1048592 | tf_op jit(solution)/shard_map/all_gather | solution.py:37
  149.2 1.3 reduce_sum.22
  150.5 0.2 convert_element_type.25
  150.7 82.0 %all-gather.8.cloned.1.call-done = bf16[64,64,512]{2,1,0:T(8,128)(2,1)} async-done(((bf16[1,64,512]{2,1,0:T(8,128)(2,1)}), bf16[64,64,512]{2,1,0:T(8,128)(2,1)}) %all-gather.8.cloned.1.call-update) | async-done | bytes 4194320 | tf_op jit(solution)/shard_map/all_gather | solution.py:46
  232.7 2.8 convolution_convert_fusion
  235.6 2.0 gather_fusion
  237.5 43.8 %reduce-scatter.2.cloned.1.call-done = f32[512,512]{1,0:T(8,128)} async-done(((f32[512,2048]{1,0:T(8,128)}), f32[512,512]{1,0:T(8,128)}) %reduce-scatter.2.cloned.1.call-update) | async-done | bytes 1048592 | tf_op jit(solution)/shard_map/reduce_scatter | solution.py:29
  281.4 2.2 add_convert_fusion
  (7 shorter events, 0.1 us)
Async XLA Ops:
  6.5 107.8 %all-gather.4.cloned.1.call-start = ((), (), s32[]{:S(2)}) async-start(), calls=%async_computation.2 | async-start | bytes 17039360 | tf_op jit(solution)/shard_map/all_gather | solution.py:33
  7.3 141.9 %all-gather.6.cloned.1.call-start = ((), (), s32[]{:S(2)}) async-start(), calls=%async_computation.3 | async-start | bytes 1310720 | tf_op jit(solution)/shard_map/all_gather | solution.py:37
  114.3 13.5 %copy-start = (bf16[512,2048]{1,0:T(8,128)(2,1)S(1)}, bf16[512,2048]{1,0:T(8,128)(2,1)}, u32[]{:S(2)}) copy-start(bf16[512,2048]{1,0:T(8,128)(2,1)} %param.5) | copy-start | bytes 6291460
  126.9 105.8 %all-gather.8.cloned.1.call-start = ((), (), s32[]{:S(2)}) async-start(), calls=%async_computation.4 | async-start | bytes 4259840 | tf_op jit(solution)/shard_map/all_gather | solution.py:46
  127.6 153.8 %reduce-scatter.2.cloned.1.call-start = ((), (), s32[]{:S(2)}) async-start(), calls=%async_computation.1 | async-start | bytes 5242880 | tf_op jit(solution)/shard_map/reduce_scatter | solution.py:29
Sparse Core Ops, SparseCore 0:
  10.1 104.1 all-gather.3
  127.0 22.1 all-gather.5
  152.0 80.6 all-gather.7
  235.1 46.2 reduce-scatter.1

commit v2 on v0

--- a/solution.py
+++ b/solution.py
@@ -30,7 +30,10 @@
     product = jnp.einsum(
         "acd,ard->acr",
         send_buffer,
-        lax.all_gather(adapter_down_weight, "dp", axis=0, tiled=True),
+        jnp.concatenate(
+            lax.all_to_all(jnp.stack([adapter_down_weight] * lax.axis_size("dp")), "dp", 0, 0),
+            axis=0,
+        ),
         preferred_element_type=jnp.float32,
     )
     summed = lax.psum(product.reshape(holder_count, row_capacity * adapter_rank_width), "tensor")

time: 209 us -> 458 us (2.19)
  the two profiles are of different devices: /device:TPU:1 before, /device:TPU:48 now
where the time goes in v2:
time: 458 us; the launch traced here: 457 us
  waiting for transfers between devices  367 us (80%)
  matrix products  23.8 us (5%)
  blocking collectives  20 us (4%)
  local copies, waits for them, and re-layouts  16.1 us (4%)
  between operations  14.9 us (3%)
  starting transfers between devices  11.9 us (3%)
    all_to_all x1, waiting for transfers between devices, on_device(): lax.all_to_all(jnp.stack([adapter_down_weight] * lax.axis_size('dp')), 'd...  366 us
    psum x1, blocking collectives, on_device(): lax.psum(product.reshape(holder_count, row_capacity * adapter_rank_width)...  20 us
    all_to_all x1, starting transfers between devices, on_device(): lax.all_to_all(jnp.stack([adapter_down_weight] * lax.axis_size('dp')), 'd...  11.9 us
    dot_general x1, matrix products, on_device(): jnp.einsum('acd,ard->acr', send_buffer, jnp.concatenate(lax.all_to_all(jn...  11.5 us
    dot_general x1, matrix products, on_device(): jnp.dot(tokens, frozen_key_value_weight, preferred_element_type=jnp.float32)  9.44 us
  transfers between devices with their start and end apart: 3, of which 1 were waited for; matrix products, arithmetic and copies ran while one was open for 7% of the time, Pallas kernels for 0%

profile of v2, /device:TPU:48, one launch (start us, length us, event | category | flops | bytes accessed | tf_op | source)
XLA Modules:
  0.0 457.2 jit_solution(5055019261513162043)
XLA Ops:
  7.4 6.7 %stack.2 = bf16[64,1,64,2048]{3,2,1,0:T(8,128)(2,1)} broadcast(bf16[64,2048]{1,0:T(8,128)(2,1)} %bitcast.36), dimensions={2,3} | broadcast | bytes 17039360 | tf_op jit(solution)/shard_map/stack | solution.py:34
  14.1 11.9 %all-to-all-start = ((bf16[64,1,64,2048]{3,2,1,0:T(8,128)(2,1)}), bf16[64,1,64,2048]{3,2,1,0:T(8,128)(2,1)}, u32[]{:S(2)}, u32[]{:S(2)}) async-start(bf16[64,1,64,2048]{3,2,1,0:T(8,128)(2,1)} %stack.2), calls=%async_computation.1 | async-start | bytes 33554432 | tf_op jit(solution)/shard_map/all_to_all | solution.py:34
  25.9 0.0 all-gather.2.cloned.1.call-start
  26.0 0.7 all-gather.2.cloned.1.call-update
  26.7 0.0 reduce-scatter.2.cloned.1.call-start
  26.7 0.0 copy-done.1
  26.7 9.4 %fusion.8 = f32[512,2048]{1,0:T(8,128)} fusion(bf16[512,2048]{1,0:T(8,128)(2,1)S(1)} %copy-done.1, bf16[2048,2048]{1,0:T(8,128)(2,1)} %param.7), kind=kOutput, calls=%fused_computation.19 | convolution fusion | flops 4294967296 | bytes 14680064 | tf_op jit(solution)/shard_map/dot_general | solution.py:28
  36.2 0.0 copy-start
  36.2 0.0 reduce-scatter.2.cloned.1.call-update
  36.2 0.7 copy-done
  36.9 1.2 reduce-window.6
  38.1 0.2 slice_reduce_fusion
  38.3 0.1 fusion.6
  38.5 6.2 %scatter_custom_fusion = bf16[1024,2048]{1,0:T(8,128)(2,1)} fusion(s32[512]{0:T(512)S(1)} %bitcast.40, bf16[512,2048]{1,0:T(8,128)(2,1)S(1)} %copy-done.1, bf16[]{:T(256)} %constant.4.clone.1), kind=kCustom, calls=%fused_computation.4 | custom fusion | bytes 4194306 | tf_op jit(solution)/shard_map/scatter | solution.py:25
  44.6 366.1 %all-to-all-done = bf16[64,1,64,2048]{3,2,1,0:T(8,128)(2,1)} async-done(((bf16[64,1,64,2048]{3,2,1,0:T(8,128)(2,1)}), bf16[64,1,64,2048]{3,2,1,0:T(8,128)(2,1)}, u32[]{:S(2)}, u32[]{:S(2)}) %all-to-all-start) | async-done | bytes 16777248 | tf_op jit(solution)/shard_map/all_to_all | solution.py:34
  410.8 11.5 %fusion = f32[64,16,64]{2,1,0:T(8,128)S(1)} fusion(bf16[64,16,2048]{2,1,0:T(8,128)(2,1)} %bitcast.35, bf16[64,1,64,2048]{3,2,1,0:T(8,128)(2,1)} %all-to-all-done), kind=kOutput, calls=%fused_computation.2 | convolution fusion | flops 268435456 | bytes 21233664 | tf_op jit(solution)/shard_map/acd,ard->acr/dot_general | solution.py:30
  422.3 0.2 reshape.37
  422.5 20.0 %all-reduce.1 = bf16[64,1024]{1,0:T(8,128)(2,1)S(1)} all-reduce(f32[64,1024]{1,0:T(8,128)S(1)} %reshape.37), channel_id=1, replica_groups=mesh['dp'=64,'tensor'=4] {'tensor'}, use_global_device_ids=true, to_apply=%region_5.6 | all-reduce | flops 65536 | bytes 393216 | tf_op jit(solution)/shard_map/psum | solution.py:39
  442.5 0.2 convert_element_type.25
  442.6 0.0 all-gather.2.cloned.1.call-done
  442.7 2.8 convolution_convert_fusion
  445.5 2.0 gather_fusion
  447.5 0.0 reduce-scatter.2.cloned.1.call-done
  447.5 2.2 add_convert_fusion
  (6 shorter events, 0.1 us)
Async XLA Ops:
  14.1 12.7 %copy-start.1 = (bf16[512,2048]{1,0:T(8,128)(2,1)S(1)}, bf16[512,2048]{1,0:T(8,128)(2,1)}, u32[]{:S(2)}) copy-start(bf16[512,2048]{1,0:T(8,128)(2,1)} %param.5) | copy-start | bytes 6291460
  14.1 396.7 %all-to-all-start = ((bf16[64,1,64,2048]{3,2,1,0:T(8,128)(2,1)}), bf16[64,1,64,2048]{3,2,1,0:T(8,128)(2,1)}, u32[]{:S(2)}, u32[]{:S(2)}) async-start(bf16[64,1,64,2048]{3,2,1,0:T(8,128)(2,1)} %stack.2), calls=%async_computation.1 | async-start | bytes 33554432 | tf_op jit(solution)/shard_map/all_to_all | solution.py:34
  25.9 416.7 %all-gather.2.cloned.1.call-start = ((), (), s32[]{:S(2)}) async-start(), calls=%async_computation.3 | async-start | bytes 4259840 | tf_op jit(solution)/shard_map/all_gather | solution.py:46
  26.7 420.9 %reduce-scatter.2.cloned.1.call-start = ((), (), s32[]{:S(2)}) async-start(), calls=%async_computation.2 | async-start | bytes 5242880 | tf_op jit(solution)/shard_map/reduce_scatter | solution.py:29
  36.2 0.7 copy-start
Sparse Core Ops, SparseCore 0:
  29.9 145.4 all-gather.1
Sparse Core Ops, SparseCore 1:
  36.3 50.4 reduce-scatter.1
